TPU v7x, 256 devices: a whole 4x4x8 slice. The times are simulated.
256 devices in a mesh: grid: 32 (over z, y), var: 8 (over x, core).
Axes of the slice: x: 4, y: 4, z: 8, core: 2. Of those that a mesh axis runs over, the one named last changes fastest.
Arguments:
- data: bfloat16 [8, 1024, 49152], P('var', None, 'grid'), may hold values from -6 to 6
- area: float32 [49152], P('grid'), may hold values from 0.1 to 1
- eofs: bfloat16 [8, 49152, 128], P('var', 'grid'), may hold values from -0.02734375 to 0.02734375
- var_scale: float32 [8], P('var'), may hold values from 0.5 to 2
- recon_map: bfloat16 [8, 1024, 49152], P('var', None, 'grid'), may hold values from -0.1875 to 0.1875
Outputs:
- fields: bfloat16 [8, 1024, 49152], P('var', None, 'grid')
All inputs are finite; a program needn't handle non-finite values.
Results may differ from a plain program's by a relative error of at most 0.0057.
Values may be sent and summed in bfloat16 or wider, within the bound.
No kernel may reach another device: no remote copies, remote signals or barrier semaphores. Data moves between devices by JAX's collectives and lax.ppermute only.
A program may use at most 64 MiB of HBM per device.

v0:
```python
import jax
import jax.numpy as jnp
from jax import lax
from jax.sharding import PartitionSpec as P


def body(data, area, eofs, var_scale, recon_map):
    scaled = (area[:, None] * eofs[0].astype(jnp.float32)).astype(jnp.bfloat16)
    partial_comps = jnp.dot(data[0], scaled, preferred_element_type=jnp.float32)
    comps = lax.psum(partial_comps, "grid")
    joined_local = (var_scale[0] * comps).astype(jnp.bfloat16)
    patterns = recon_map[0]
    rebuilt = jnp.dot(
        lax.all_gather(joined_local, "var", axis=1, tiled=True),
        patterns,
        preferred_element_type=jnp.float32,
    )
    return rebuilt.astype(jnp.bfloat16)[None]


def solution(mesh):
    placed = (
        P("var", None, "grid"),
        P("grid"),
        P("var", "grid", None),
        P("var"),
        P("var", None, "grid"),
    )
    return jax.shard_map(
        body, mesh=mesh, in_specs=placed, out_specs=P("var", None, "grid"), check_vma=False
    )
```

profile of v0, /device:TPU:1, one launch (start us, length us, event | category | flops | bytes accessed | tf_op | source)
XLA Modules:
  0.0 204.4 jit_solution(12069375334948118248)
XLA Ops:
  6.5 0.0 copy-start
  6.5 0.0 all-reduce.2.cloned.1.call-start
  6.5 4.0 %fusion.4 = f32[1024,128]{1,0:T(8,128)} fusion(bf16[1,1024,1536]{2,1,0:T(8,128)(2,1)} %param.5, bf16[1,1536,128]{2,1,0:T(8,128)(2,1)} %param.7, f32[1536]{0:T(1024)} %param.6), kind=kOutput, calls=%fused_computation.5 | convolution fusion | flops 403243008 | bytes 4069376 | tf_op jit(solution)/shard_map/dot_general | solution.py:9
  10.6 0.0 all-reduce.2.cloned.1.call-update
  10.6 0.0 all-gather.2.cloned.1.call-start
  11.3 146.2 %all-reduce.2.cloned.1.call-done = f32[1024,128]{1,0:T(8,128)} async-done(((f32[1024,128]{1,0:T(8,128)}), f32[1024,128]{1,0:T(8,128)}) %all-reduce.2.cloned.1.call-update) | async-done | bytes 524304 | tf_op jit(solution)/shard_map/psum | solution.py:10
  157.5 1.8 multiply_convert_fusion.1
  159.3 0.0 all-gather.2.cloned.1.call-update
  159.3 31.9 %all-gather.2.cloned.1.call-done = bf16[1024,1024]{1,0:T(8,128)(2,1)} async-done(((bf16[1024,128]{1,0:T(8,128)(2,1)}), bf16[1024,1024]{1,0:T(8,128)(2,1)}) %all-gather.2.cloned.1.call-update) | async-done | bytes 2097168 | tf_op jit(solution)/shard_map/all_gather | solution.py:14
  191.2 0.0 copy-done
  191.2 6.3 %fusion = bf16[1,1024,1536]{2,1,0:T(8,128)(2,1)} fusion(bf16[1024,1024]{1,0:T(8,128)(2,1)} %all-gather.2.cloned.1.call-done, bf16[1,1024,1536]{2,1,0:T(8,128)(2,1)S(1)} %copy-done), kind=kOutput, calls=%fused_computation.1 | convolution fusion | flops 3222798336 | bytes 8388608 | tf_op jit(solution)/shard_map/dot_general | solution.py:13
Async XLA Ops:
  6.5 184.7 %copy-start = (bf16[1,1024,1536]{2,1,0:T(8,128)(2,1)S(1)}, bf16[1,1024,1536]{2,1,0:T(8,128)(2,1)}, u32[]{:S(2)}) copy-start(bf16[1,1024,1536]{2,1,0:T(8,128)(2,1)} %param.9) | copy-start | bytes 9437188
  6.5 151.0 %all-reduce.2.cloned.1.call-start = ((), (), s32[]{:S(2)}) async-start(), calls=%async_computation | async-start | bytes 1048576 | tf_op jit(solution)/shard_map/psum | solution.py:10
  10.6 180.6 %all-gather.2.cloned.1.call-start = ((), (), s32[]{:S(2)}) async-start(), calls=%async_computation.1 | async-start | bytes 2359296 | tf_op jit(solution)/shard_map/all_gather | solution.py:14
Sparse Core Ops, SparseCore 0:
  10.8 146.7 all-reduce.1
  159.5 31.6 all-gather.1
where the time goes:
time: 205 us; the launch traced here: 204 us
  waiting for transfers between devices  178 us (87%)
  between operations  14 us (7%)
  matrix products  10.4 us (5%)
    psum x1, waiting for transfers between devices, body(): comps = lax.psum(partial_comps, 'grid')  146 us
    all_gather x1, waiting for transfers between devices, body(): lax.all_gather(joined_local, 'var', axis=1, tiled=True)  31.9 us
    dot_general x1, matrix products, body(): jnp.dot(lax.all_gather(joined_local, 'var', axis=1, tiled=True), patterns...  6.35 us
  transfers between devices with their start and end apart: 2, of which 2 were waited for; matrix products, arithmetic and copies ran while one was open for 0% of the time, Pallas kernels for 0%

commit v1 on v0

--- a/solution.py
+++ b/solution.py
@@ -7,7 +7,9 @@
 def body(data, area, eofs, var_scale, recon_map):
     scaled = (area[:, None] * eofs[0].astype(jnp.float32)).astype(jnp.bfloat16)
     partial_comps = jnp.dot(data[0], scaled, preferred_element_type=jnp.float32)
-    comps = lax.psum(partial_comps, "grid")
+    comps = partial_comps
+    for hop in (1, 2, 4, 8, 16):
+        comps = comps + lax.ppermute(comps, "grid", [(dev, dev ^ hop) for dev in range(32)])
     joined_local = (var_scale[0] * comps).astype(jnp.bfloat16)
     patterns = recon_map[0]
     rebuilt = jnp.dot(

time: 205 us -> 146 us (0.71)
  waiting for transfers between devices: 178 us -> 103 us
  starting transfers between devices: 0.04 us -> 17.6 us
    psum x1 -> x0, waiting for transfers between devices: 146 us -> none  [body(): comps = lax.psum(partial_comps, 'grid')]
    ppermute x0 -> x5, waiting for transfers between devices: none -> 75 us  [body(): lax.ppermute(comps, 'grid', [(dev, dev ^ hop) for dev in range(32)])]
    ppermute x0 -> x5, starting transfers between devices: none -> 17.6 us  [body(): lax.ppermute(comps, 'grid', [(dev, dev ^ hop) for dev in range(32)])]
    all_gather x1, waiting for transfers between devices: 31.9 us -> 28.5 us  [body(): lax.all_gather(joined_local, 'var', axis=1, tiled=True)]
  transfers between devices with their start and end apart: 2 -> 6, of which waited for: 2 -> 6; matrix products, arithmetic and copies ran while one was open for 0% -> 0% of each run, Pallas kernels for 0% -> 0%
where the time goes in v1:
time: 146 us
  waiting for transfers between devices  103 us (71%)
  starting transfers between devices  17.6 us (12%)
  between operations  14.1 us (10%)
  matrix products  10.2 us (7%)
    ppermute x5, waiting for transfers between devices, body(): lax.ppermute(comps, 'grid', [(dev, dev ^ hop) for dev in range(32)])  75 us
    all_gather x1, waiting for transfers between devices, body(): lax.all_gather(joined_local, 'var', axis=1, tiled=True)  28.5 us
    ppermute x5, starting transfers between devices, body(): lax.ppermute(comps, 'grid', [(dev, dev ^ hop) for dev in range(32)])  17.6 us
    dot_general x1, matrix products, body(): jnp.dot(lax.all_gather(joined_local, 'var', axis=1, tiled=True), patterns...  6.51 us
    dot_general x1, matrix products, body(): partial_comps = jnp.dot(data[0], scaled, preferred_element_type=jnp.float32)  3.67 us
  transfers between devices with their start and end apart: 6, of which 6 were waited for; matrix products, arithmetic and copies ran while one was open for 0% of the time, Pallas kernels for 0%

profile of v1, /device:TPU:1, one launch (start us, length us, event | category | flops | bytes accessed | tf_op | source)
XLA Modules:
  0.0 146.3 jit_solution(14670565604478909006)
XLA Ops:
  6.5 0.0 copy-start
  6.5 0.0 all-gather.2.cloned.1.call-start
  6.5 3.7 %fusion.4 = f32[1024,128]{0,1:T(8,128)S(1)} fusion(bf16[1,1024,1536]{2,1,0:T(8,128)(2,1)} %param.5, bf16[1,1536,128]{2,1,0:T(8,128)(2,1)} %param.7, f32[1536]{0:T(1024)} %param.6), kind=kOutput, calls=%fused_computation.5 | convolution fusion | flops 403243008 | bytes 4069376 | tf_op jit(solution)/shard_map/dot_general | solution.py:9
  10.2 2.2 %collective-permute-start = (f32[1024,128]{0,1:T(8,128)S(1)}, f32[1024,128]{0,1:T(8,128)S(1)}, u32[]{:S(2)}, u32[]{:S(2)}) collective-permute-start(f32[1024,128]{0,1:T(8,128)S(1)} %fusion.4), channel_id=1, source_target_pairs={{0,8},{8,0},{16,24},{24,16},{32,40},{40,32},{48,56},{56,48},{64,72... | collective-permute-start | bytes 1572872 | tf_op jit(solution)/shard_map/ppermute | solution.py:12
  12.4 10.4 %collective-permute-done = f32[1024,128]{0,1:T(8,128)S(1)} collective-permute-done((f32[1024,128]{0,1:T(8,128)S(1)}, f32[1024,128]{0,1:T(8,128)S(1)}, u32[]{:S(2)}, u32[]{:S(2)}) %collective-permute-start) | collective-permute-done | bytes 524320 | tf_op jit(solution)/shard_map/ppermute | solution.py:12
  22.8 0.1 add.15
  22.9 4.1 %collective-permute-start.1 = (f32[1024,128]{0,1:T(8,128)S(1)}, f32[1024,128]{0,1:T(8,128)S(1)}, u32[]{:S(2)}, u32[]{:S(2)}) collective-permute-start(f32[1024,128]{0,1:T(8,128)S(1)} %add.15), channel_id=1, source_target_pairs={{0,16},{8,24},{16,0},{24,8},{32,48},{40,56},{48,32},{56,40},{64,80... | collective-permute-start | bytes 1572872 | tf_op jit(solution)/shard_map/ppermute | solution.py:12
  27.0 10.5 %collective-permute-done.1 = f32[1024,128]{0,1:T(8,128)S(1)} collective-permute-done((f32[1024,128]{0,1:T(8,128)S(1)}, f32[1024,128]{0,1:T(8,128)S(1)}, u32[]{:S(2)}, u32[]{:S(2)}) %collective-permute-start.1) | collective-permute-done | bytes 524320 | tf_op jit(solution)/shard_map/ppermute | solution.py:12
  37.5 0.1 add.16
  37.6 1.7 %collective-permute-start.2 = (f32[1024,128]{0,1:T(8,128)S(1)}, f32[1024,128]{0,1:T(8,128)S(1)}, u32[]{:S(2)}, u32[]{:S(2)}) collective-permute-start(f32[1024,128]{0,1:T(8,128)S(1)} %add.16), channel_id=1, source_target_pairs={{0,32},{8,40},{16,48},{24,56},{32,0},{40,8},{48,16},{56,24},{64,96... | collective-permute-start | bytes 1572872 | tf_op jit(solution)/shard_map/ppermute | solution.py:12
  39.2 9.7 %collective-permute-done.2 = f32[1024,128]{0,1:T(8,128)S(1)} collective-permute-done((f32[1024,128]{0,1:T(8,128)S(1)}, f32[1024,128]{0,1:T(8,128)S(1)}, u32[]{:S(2)}, u32[]{:S(2)}) %collective-permute-start.2) | collective-permute-done | bytes 524320 | tf_op jit(solution)/shard_map/ppermute | solution.py:12
  48.9 0.1 add.17
  49.0 3.1 %collective-permute-start.3 = (f32[1024,128]{0,1:T(8,128)S(1)}, f32[1024,128]{0,1:T(8,128)S(1)}, u32[]{:S(2)}, u32[]{:S(2)}) collective-permute-start(f32[1024,128]{0,1:T(8,128)S(1)} %add.17), channel_id=1, source_target_pairs={{0,64},{8,72},{16,80},{24,88},{32,96},{40,104},{48,112},{56,120},{... | collective-permute-start | bytes 1572872 | tf_op jit(solution)/shard_map/ppermute | solution.py:12
  52.1 22.4 %collective-permute-done.3 = f32[1024,128]{0,1:T(8,128)S(1)} collective-permute-done((f32[1024,128]{0,1:T(8,128)S(1)}, f32[1024,128]{0,1:T(8,128)S(1)}, u32[]{:S(2)}, u32[]{:S(2)}) %collective-permute-start.3) | collective-permute-done | bytes 524320 | tf_op jit(solution)/shard_map/ppermute | solution.py:12
  74.5 0.1 add.18
  74.6 6.6 %collective-permute-start.4 = (f32[1024,128]{0,1:T(8,128)S(1)}, f32[1024,128]{0,1:T(8,128)S(1)}, u32[]{:S(2)}, u32[]{:S(2)}) collective-permute-start(f32[1024,128]{0,1:T(8,128)S(1)} %add.18), channel_id=1, source_target_pairs={{0,128},{8,136},{16,144},{24,152},{32,160},{40,168},{48,176},{56,1... | collective-permute-start | bytes 1572872 | tf_op jit(solution)/shard_map/ppermute | solution.py:12
  81.8 21.9 %collective-permute-done.4 = f32[1024,128]{0,1:T(8,128)S(1)} collective-permute-done((f32[1024,128]{0,1:T(8,128)S(1)}, f32[1024,128]{0,1:T(8,128)S(1)}, u32[]{:S(2)}, u32[]{:S(2)}) %collective-permute-start.4) | collective-permute-done | bytes 524320 | tf_op jit(solution)/shard_map/ppermute | solution.py:12
  103.7 0.8 multiply_convert_fusion.1
  104.5 0.0 all-gather.2.cloned.1.call-update
  104.5 28.5 %all-gather.2.cloned.1.call-done = bf16[1024,1024]{0,1:T(8,128)(2,1)} async-done(((bf16[1024,128]{0,1:T(8,128)(2,1)}), bf16[1024,1024]{0,1:T(8,128)(2,1)}) %all-gather.2.cloned.1.call-update) | async-done | bytes 2097168 | tf_op jit(solution)/shard_map/all_gather | solution.py:16
  133.0 0.0 copy-done
  133.0 6.5 %fusion = bf16[1,1024,1536]{2,1,0:T(8,128)(2,1)} fusion(bf16[1024,1024]{0,1:T(8,128)(2,1)} %all-gather.2.cloned.1.call-done, bf16[1,1024,1536]{2,1,0:T(8,128)(2,1)S(1)} %copy-done), kind=kOutput, calls=%fused_computation.1 | convolution fusion | flops 3222798336 | bytes 8388608 | tf_op jit(solution)/shard_map/dot_general | solution.py:15
Async XLA Ops:
  6.5 126.5 %copy-start = (bf16[1,1024,1536]{2,1,0:T(8,128)(2,1)S(1)}, bf16[1,1024,1536]{2,1,0:T(8,128)(2,1)}, u32[]{:S(2)}) copy-start(bf16[1,1024,1536]{2,1,0:T(8,128)(2,1)} %param.9) | copy-start | bytes 9437188
  6.5 126.5 %all-gather.2.cloned.1.call-start = ((), (), s32[]{:S(2)}) async-start(), calls=%async_computation | async-start | bytes 2359296 | tf_op jit(solution)/shard_map/all_gather | solution.py:16
  10.2 12.6 %collective-permute-start = (f32[1024,128]{0,1:T(8,128)S(1)}, f32[1024,128]{0,1:T(8,128)S(1)}, u32[]{:S(2)}, u32[]{:S(2)}) collective-permute-start(f32[1024,128]{0,1:T(8,128)S(1)} %fusion.4), channel_id=1, source_target_pairs={{0,8},{8,0},{16,24},{24,16},{32,40},{40,32},{48,56},{56,48},{64,72... | collective-permute-start | bytes 1572872 | tf_op jit(solution)/shard_map/ppermute | solution.py:12
  22.9 14.6 %collective-permute-start.1 = (f32[1024,128]{0,1:T(8,128)S(1)}, f32[1024,128]{0,1:T(8,128)S(1)}, u32[]{:S(2)}, u32[]{:S(2)}) collective-permute-start(f32[1024,128]{0,1:T(8,128)S(1)} %add.15), channel_id=1, source_target_pairs={{0,16},{8,24},{16,0},{24,8},{32,48},{40,56},{48,32},{56,40},{64,80... | collective-permute-start | bytes 1572872 | tf_op jit(solution)/shard_map/ppermute | solution.py:12
  37.6 11.4 %collective-permute-start.2 = (f32[1024,128]{0,1:T(8,128)S(1)}, f32[1024,128]{0,1:T(8,128)S(1)}, u32[]{:S(2)}, u32[]{:S(2)}) collective-permute-start(f32[1024,128]{0,1:T(8,128)S(1)} %add.16), channel_id=1, source_target_pairs={{0,32},{8,40},{16,48},{24,56},{32,0},{40,8},{48,16},{56,24},{64,96... | collective-permute-start | bytes 1572872 | tf_op jit(solution)/shard_map/ppermute | solution.py:12
  49.0 25.5 %collective-permute-start.3 = (f32[1024,128]{0,1:T(8,128)S(1)}, f32[1024,128]{0,1:T(8,128)S(1)}, u32[]{:S(2)}, u32[]{:S(2)}) collective-permute-start(f32[1024,128]{0,1:T(8,128)S(1)} %add.17), channel_id=1, source_target_pairs={{0,64},{8,72},{16,80},{24,88},{32,96},{40,104},{48,112},{56,120},{... | collective-permute-start | bytes 1572872 | tf_op jit(solution)/shard_map/ppermute | solution.py:12
  74.6 29.2 %collective-permute-start.4 = (f32[1024,128]{0,1:T(8,128)S(1)}, f32[1024,128]{0,1:T(8,128)S(1)}, u32[]{:S(2)}, u32[]{:S(2)}) collective-permute-start(f32[1024,128]{0,1:T(8,128)S(1)} %add.18), channel_id=1, source_target_pairs={{0,128},{8,136},{16,144},{24,152},{32,160},{40,168},{48,176},{56,1... | collective-permute-start | bytes 1572872 | tf_op jit(solution)/shard_map/ppermute | solution.py:12
Sparse Core Ops, SparseCore 0:
  104.6 28.3 all-gather.1
